TPU v7x, 256 devices: a whole 4x4x8 slice. The times are simulated.
256 devices in a mesh: owner: 64 (over z, x, core), col: 4 (over y).
Axes of the slice: x: 4, y: 4, z: 8, core: 2. Of those that a mesh axis runs over, the one named last changes fastest.
Arguments:
- momentum: float32 [128, 512, 2048], P(None, 'owner', 'col'), may hold values from -7200 to 7200
- hidden_acts: bfloat16 [32768, 512], P('owner'), may hold values from -6 to 6
- output_grads: bfloat16 [32768, 2048], P('owner', 'col'), may hold values from -6 to 6
- routing: int32 [32768], P('owner'), may hold values from 0 to 1
- assignment: int32 [128], replicated, may hold values from 0 to 127, each once
Outputs:
- new_momentum: float32 [128, 512, 2048], P(None, 'owner', 'col')
- update: float32 [128, 512, 2048], P('owner', None, 'col')
Inputs may be any that keep to these rules, and one draw needn't show every extreme that they name: `routing`: the row's expert as a local slot of the owner group that holds the row. `assignment`: a permutation: each expert is held in exactly one slot.
All inputs are finite; a program needn't handle non-finite values.
Results may differ from a plain program's by a relative error of at most 0.0065.
Values may be sent and summed in bfloat16 or wider, within the bound.
A program may use at most 64 MiB of HBM per device.

v0:
```python
import jax
import jax.numpy as jnp
from jax import lax
from jax.sharding import Mesh
from jax.sharding import PartitionSpec as P

D = 2048
FFE = 512
EXP_DEV = 2
NS_ITERS = 2
OWNER = ("owner_0", "owner_1", "owner_2")
decay_rate = 0.95
epsilon = 1e-07
linear_weight = 3.4445
cubic_weight = -4.775
quintic_weight = 2.0315


def from_everyone(array, axis):
    copies = jnp.broadcast_to(array, (lax.axis_size(axis), *array.shape))
    return lax.all_to_all(copies, axis, split_axis=0, concat_axis=0, tiled=True)


def taken_together(array, axis):
    return from_everyone(array, axis).sum(axis=0)


def split_up(array, dim, size):
    shape = array.shape
    parts = array.reshape(*shape[:dim], size, shape[dim] // size, *shape[dim + 1 :])
    return jnp.moveaxis(parts, dim, 0)


def laid_out(parts, dim):
    shape = list(parts.shape[1:])
    shape[dim] *= parts.shape[0]
    return jnp.moveaxis(parts, 0, dim).reshape(shape)


def turned_blocks(parts, axes, sequence):
    shape = [lax.axis_size(a) for a in axes]
    parts = parts.reshape(*shape, *parts.shape[1:])
    for k in sequence:
        parts = lax.all_to_all(parts, axes[k], split_axis=k, concat_axis=k, tiled=True)
    return parts.reshape(-1, *parts.shape[len(axes) :])


def core_and_chips(array, groups, sequence, split_dim, concat_dim):
    size = lax.axis_size(groups[0]) * lax.axis_size(groups[1])
    parts = split_up(array, split_dim, size)
    return laid_out(turned_blocks(parts, groups, sequence), concat_dim)


def newton_turn(iterate, gram_matrix):
    square = jnp.einsum(
        "jfg,jgh->jfh", gram_matrix, gram_matrix, preferred_element_type=jnp.float32
    )
    polynomial = (cubic_weight * gram_matrix.astype(jnp.float32) + quintic_weight * square).astype(
        jnp.bfloat16
    )
    product = jnp.einsum("jfg,jgd->jfd", polynomial, iterate, preferred_element_type=jnp.float32)
    return (linear_weight * iterate.astype(jnp.float32) + product).astype(jnp.bfloat16)


def body(momentum, hidden_acts, output_grads, routing, assignment):
    scaling = 0.2 * float(max(FFE, D)) ** 0.5
    columns = output_grads.shape[1]
    ordered = jnp.take(momentum, assignment, axis=0)
    received = lax.all_to_all(ordered, OWNER, split_axis=0, concat_axis=1, tiled=True)
    slot_ids = jnp.arange(EXP_DEV, dtype=jnp.int32)
    selected = routing[:, None, None] == slot_ids[None, :, None]
    masked = jnp.where(selected, output_grads[:, None, :], jnp.zeros((), jnp.bfloat16))
    gradient = jnp.einsum("rf,rjd->jfd", hidden_acts, masked, preferred_element_type=jnp.float32)
    updated = decay_rate * received + gradient
    squares = taken_together(jnp.sum(updated * updated, axis=(1, 2)), "col")
    iterate = (updated / (jnp.sqrt(squares)[:, None, None] + epsilon)).astype(jnp.bfloat16)
    complete = lax.all_gather(iterate, "col", axis=2, tiled=True)
    for turn_index in range(NS_ITERS):
        gram_matrix = jnp.einsum(
            "jfd,jgd->jfg", complete, complete, preferred_element_type=jnp.float32
        ).astype(jnp.bfloat16)
        complete = newton_turn(complete, gram_matrix)
    result_cols = lax.dynamic_slice_in_dim(complete, lax.axis_index("col") * columns, columns, 2)
    update = scaling * result_cols.astype(jnp.float32)
    returned = core_and_chips(
        updated.astype(jnp.bfloat16), (("owner_0", "owner_1"), "owner_2"), (1, 0), 1, 0
    ).astype(updated.dtype)
    new_momentum = jnp.zeros_like(momentum).at[assignment].set(returned)
    return (new_momentum, update)


def solution(mesh):
    torus = Mesh(
        mesh.devices.reshape(8, 4, 2, mesh.shape["col"]), ("owner_0", "owner_1", "owner_2", "col")
    )
    return jax.shard_map(
        body,
        mesh=torus,
        in_specs=(P(None, OWNER, "col"), P(OWNER, None), P(OWNER, "col"), P(OWNER), P()),
        out_specs=(P(None, OWNER, "col"), P(OWNER, None, "col")),
        check_vma=False,
    )
```

profile of v0, /device:TPU:2, one launch (start us, length us, event | category | flops | bytes accessed | tf_op | source)
XLA Modules:
  0.0 192.8 jit_solution(2016149358250970594)
XLA Ops:
  7.2 0.8 compare_select_fusion
  8.0 0.7 compare_and_fusion
  8.7 0.1 copy-done
  8.8 2.1 %gather_fusion = f32[128,8,512]{2,1,0:T(8,128)} fusion(f32[128,8,512]{2,1,0:T(8,128)S(1)} %copy-done, s32[1024]{0:T(1024)S(1)} %pad_clamp_fusion), kind=kCustom, calls=%fused_computation | custom fusion | bytes 4194816 | tf_op jit(solution)/shard_map/jit(_take)/gather | solution.py:68
  10.9 3.1 %broadcast_select_fusion = f32[128,8,512]{2,1,0:T(8,128)} fusion(f32[128,8,512]{2,1,0:T(8,128)} %gather_fusion, pred[128]{0:T(512)(128)(4,1)S(1)} %compare_and_fusion), kind=kLoop, calls=%fused_computation.16 | loop fusion | flops 524288 | bytes 4194432 | tf_op jit(solution)/shard_map/jit(_take)/select_n | solution.py:68
  14.0 12.3 %all-to-all-start = ((f32[128,8,512]{2,1,0:T(8,128)}), f32[128,8,512]{2,1,0:T(8,128)}, u32[]{:S(2)}, u32[]{:S(2)}) async-start(f32[128,8,512]{2,1,0:T(8,128)} %broadcast_select_fusion), calls=%async_computation | async-start | bytes 4194304 | tf_op jit(solution)/shard_map/all_to_all | solution.py:69
  26.4 51.1 %all-to-all-done = f32[128,8,512]{2,1,0:T(8,128)} async-done(((f32[128,8,512]{2,1,0:T(8,128)}), f32[128,8,512]{2,1,0:T(8,128)}, u32[]{:S(2)}, u32[]{:S(2)}) %all-to-all-start) | async-done | bytes 2097184 | tf_op jit(solution)/shard_map/all_to_all | solution.py:69
  77.5 1.9 broadcast_multiply_fusion
  79.4 2.2 %multiply_reduce_fusion = (f32[2]{0:T(128)S(1)}, f32[2,512,512]{2,1,0:T(8,128)}) fusion(bf16[512,512]{1,0:T(8,128)(2,1)S(1)} %copy-done.2, pred[512,2]{0,1:T(4,128)(4,1)S(1)} %iota_compare_fusion, bf16[512,512]{1,0:T(8,128)(2,1)S(1)} %copy-done.3, f32[64,2,8,512]{3,2,1,0:T(8,128)S(1)} %bitcast.31), kind=kOutput, calls=%fused_computation.10 | convolution fusion | flops 538968064 | bytes 5243912 | tf_op jit(solution)/shard_map/rf,rjd->jfd/dot_general | solution.py:73
  81.7 9.5 %all_to_all.25 = f32[4,1,2]{2,1,0:T(1,128)S(1)} all-to-all(f32[4,1,2]{2,1,0:T(1,128)S(1)} %broadcast_in_dim.50), channel_id=1, replica_groups=mesh['owner_0'=8,'owner_1'=4,'owner_2'=2,'col'=4] {'col'}, dimensions={0} | all-to-all | bytes 64 | tf_op jit(solution)/shard_map/all_to_all | solution.py:21
  91.2 3.6 %divide_convert_fusion = (bf16[2,512,512]{2,1,0:T(8,128)(2,1)}, bf16[2,512,512]{2,1,0:T(8,128)(2,1)S(1)}) fusion(f32[2,512,512]{2,1,0:T(8,128)} %get-tuple-element.5, f32[2]{0:T(128)S(1)} %sqrt_add_fusion), kind=kLoop, calls=%fused_computation.9 | loop fusion | flops 1572864 | bytes 4194312 | tf_op jit(solution)/shard_map/convert_element_type | solution.py:76
  94.9 0.2 copy.28
  95.1 4.6 %all_to_all.26 = bf16[32,2,2,8,512]{4,3,2,0,1:T(8,128)(2,1)S(1)} all-to-all(bf16[32,2,2,8,512]{4,3,2,0,1:T(8,128)(2,1)S(1)} %copy.28), channel_id=1, replica_groups=mesh['owner_0'=8,'owner_1'=4,'owner_2'=2,'col'=4] {'owner_2'}, dimensions={1} | all-to-all | bytes 2097152 | tf_op jit(solution)/shard_map/all_to_all | solution.py:44
  99.6 1.1 copy.29
  100.7 5.0 %all-to-all-start.2 = ((bf16[32,2,2,8,512]{4,3,2,1,0:T(8,128)(2,1)}), bf16[32,2,2,8,512]{4,3,2,1,0:T(8,128)(2,1)S(1)}, u32[]{:S(2)}, u32[]{:S(2)}) async-start(bf16[32,2,2,8,512]{4,3,2,1,0:T(8,128)(2,1)} %copy.29), calls=%async_computation.2 | async-start | bytes 2097152 | tf_op jit(solution)/shard_map/all_to_all | solution.py:44
  105.8 28.4 %all-to-all-done.2 = bf16[32,2,2,8,512]{4,3,2,1,0:T(8,128)(2,1)S(1)} async-done(((bf16[32,2,2,8,512]{4,3,2,1,0:T(8,128)(2,1)}), bf16[32,2,2,8,512]{4,3,2,1,0:T(8,128)(2,1)S(1)}, u32[]{:S(2)}, u32[]{:S(2)}) %all-to-all-start.2) | async-done | bytes 1048608 | tf_op jit(solution)/shard_map/all_to_all | solution.py:44
  134.1 1.7 bitcast_convert_fusion
  135.8 1.6 broadcast_in_dim.43
  137.4 17.6 %scatter_fusion = f32[128,8,512]{2,1,0:T(8,128)} fusion(f32[128,8,512]{2,1,0:T(8,128)} %broadcast_in_dim.43, s32[128]{0:T(128)S(1)} %compare_select_fusion, f32[128,8,512]{2,1,0:T(8,128)} %bitcast_convert_fusion), kind=kCustom, calls=%fused_computation.1 | custom fusion | bytes 6291968 | tf_op jit(solution)/shard_map/scatter | solution.py:88
  155.0 5.8 %convolution_convert_fusion.1 = bf16[2,512,512]{2,1,0:T(8,128)(2,1)S(1)} fusion(bf16[2,512,2048]{2,1,0:T(8,128)(2,1)} %all-gather.2.cloned.1.call-done), kind=kOutput, calls=%fused_computation.12 | convolution fusion | flops 2148007936 | bytes 5242880 | tf_op jit(solution)/shard_map/jfd,jgd->jfg/dot_general | solution.py:79
  160.9 7.4 %add_convert_fusion = bf16[2,512,2048]{2,1,0:T(8,128)(2,1)} fusion(bf16[2,512,2048]{2,1,0:T(8,128)(2,1)} %all-gather.2.cloned.1.call-done, bf16[2,512,512]{2,1,0:T(8,128)(2,1)S(1)} %convolution_convert_fusion.1), kind=kOutput, calls=%fused_computation.2 | convolution fusion | flops 2695364608 | bytes 9437184 | tf_op jit(solution)/shard_map/jfg,jgd->jfd/dot_general | solution.py:61
  168.2 5.8 %convolution_convert_fusion = bf16[2,512,512]{2,1,0:T(8,128)(2,1)S(1)} fusion(bf16[2,512,2048]{2,1,0:T(8,128)(2,1)} %add_convert_fusion), kind=kOutput, calls=%fused_computation.11 | convolution fusion | flops 2148007936 | bytes 5242880 | tf_op jit(solution)/shard_map/jfd,jgd->jfg/dot_general | solution.py:79
  174.0 8.3 %fusion.3 = f32[2,512,2048]{2,1,0:T(8,128)} fusion(bf16[2,512,2048]{2,1,0:T(8,128)(2,1)} %add_convert_fusion, bf16[2,512,512]{2,1,0:T(8,128)(2,1)S(1)} %convolution_convert_fusion), kind=kOutput, calls=%fused_computation.18 | convolution fusion | flops 2686976000 | bytes 13631488 | tf_op jit(solution)/shard_map/jfg,jgd->jfd/dot_general | solution.py:61
  182.4 3.6 %convert_multiply_fusion = f32[2,512,512]{2,1,0:T(8,128)} fusion(f32[2,512,2048]{2,1,0:T(8,128)} %fusion.3, s32[]{:T(128)S(6)} %select_n.20, bf16[2,512,2048]{2,1,0:T(8,128)(2,1)} %add_convert_fusion), kind=kLoop, calls=%fused_computation.6 | loop fusion | flops 3145728 | bytes 5242884 | tf_op jit(solution)/shard_map/mul | solution.py:84
  (15 shorter events, 0.1 us)
Async XLA Ops:
  7.2 1.6 copy-start
  14.0 12.4 %copy-start.1 = (s32[512]{0:T(512)S(1)}, s32[512]{0:T(512)}, u32[]{:S(2)}) copy-start(s32[512]{0:T(512)} %param.8) | copy-start | bytes 6148
  14.0 63.5 %all-to-all-start = ((f32[128,8,512]{2,1,0:T(8,128)}), f32[128,8,512]{2,1,0:T(8,128)}, u32[]{:S(2)}, u32[]{:S(2)}) async-start(f32[128,8,512]{2,1,0:T(8,128)} %broadcast_select_fusion), calls=%async_computation | async-start | bytes 4194304 | tf_op jit(solution)/shard_map/all_to_all | solution.py:69
  26.4 128.7 %all-gather.2.cloned.1.call-start = ((), (), s32[]{:S(2)}) async-start(), calls=%async_computation.4 | async-start | bytes 5242880 | tf_op jit(solution)/shard_map/all_gather | solution.py:77
  26.4 53.0 %copy-start.2 = (bf16[512,512]{1,0:T(8,128)(2,1)S(1)}, bf16[512,512]{1,0:T(8,128)(2,1)}, u32[]{:S(2)}) copy-start(bf16[512,512]{1,0:T(8,128)(2,1)} %param.6) | copy-start | bytes 1572868
  77.5 1.9 copy-start.3
  100.7 33.4 %all-to-all-start.2 = ((bf16[32,2,2,8,512]{4,3,2,1,0:T(8,128)(2,1)}), bf16[32,2,2,8,512]{4,3,2,1,0:T(8,128)(2,1)S(1)}, u32[]{:S(2)}, u32[]{:S(2)}) async-start(bf16[32,2,2,8,512]{4,3,2,1,0:T(8,128)(2,1)} %copy.29), calls=%async_computation.2 | async-start | bytes 2097152 | tf_op jit(solution)/shard_map/all_to_all | solution.py:44
Sparse Core Ops, SparseCore 0:
  95.0 45.1 all-gather.1
where the time goes:
time: 193 us
  waiting for transfers between devices  79.4 us (41%)
  matrix products  29.6 us (15%)
  local copies, waits for them, and re-layouts  22.7 us (12%)
  starting transfers between devices  17.4 us (9%)
  other arithmetic  15.4 us (8%)
  blocking collectives  14.1 us (7%)
  between operations  14.1 us (7%)
    all_to_all x1, waiting for transfers between devices, body(): lax.all_to_all(ordered, OWNER, split_axis=0, concat_axis=1, tiled=True)  51.1 us
    all_to_all x1, waiting for transfers between devices, turned_blocks(): lax.all_to_all(parts, axes[k], split_axis=k, concat_axis=k, tiled=True)  28.4 us
    scatter x1, local copies, waits for them, and re-layouts, body(): new_momentum = jnp.zeros_like(momentum).at[assignment].set(returned)  17.6 us
    dot_general x2, matrix products, newton_turn(): jnp.einsum('jfg,jgd->jfd', polynomial, iterate, preferred_element_type=jn...  15.7 us
    all_to_all x1, starting transfers between devices, body(): lax.all_to_all(ordered, OWNER, split_axis=0, concat_axis=1, tiled=True)  12.3 us
    dot_general x2, matrix products, body(): jnp.einsum('jfd,jgd->jfg', complete, complete, preferred_element_type=jnp...  11.6 us
    all_to_all x1, blocking collectives, from_everyone(): return lax.all_to_all(copies, axis, split_axis=0, concat_axis=0, tiled=True)  9.54 us
    all_to_all x1, starting transfers between devices, turned_blocks(): lax.all_to_all(parts, axes[k], split_axis=k, concat_axis=k, tiled=True)  5.04 us
  transfers between devices with their start and end apart: 3, of which 2 were waited for; matrix products, arithmetic and copies ran while one was open for 11% of the time, Pallas kernels for 0%

commit v1 on v0

--- a/solution.py
+++ b/solution.py
@@ -14,6 +14,13 @@
 linear_weight = 3.4445
 cubic_weight = -4.775
 quintic_weight = 2.0315
+
+
+def exchange_blocks(value, axis, split, join):
+    count = lax.axis_size(axis)
+    blocks = jnp.stack(jnp.split(value, count, axis=split), axis=0)
+    blocks = lax.all_to_all(blocks, axis, split_axis=0, concat_axis=0)
+    return jnp.concatenate(blocks, axis=join)
 
 
 def from_everyone(array, axis):
@@ -66,7 +73,7 @@
     scaling = 0.2 * float(max(FFE, D)) ** 0.5
     columns = output_grads.shape[1]
     ordered = jnp.take(momentum, assignment, axis=0)
-    received = lax.all_to_all(ordered, OWNER, split_axis=0, concat_axis=1, tiled=True)
+    received = exchange_blocks(ordered, OWNER, 0, 1)
     slot_ids = jnp.arange(EXP_DEV, dtype=jnp.int32)
     selected = routing[:, None, None] == slot_ids[None, :, None]
     masked = jnp.where(selected, output_grads[:, None, :], jnp.zeros((), jnp.bfloat16))

time: 193 us -> 231 us (1.20)
  local copies, waits for them, and re-layouts: 22.7 us -> 62.2 us
  other arithmetic: 15.4 us -> 12.2 us
    unnamed x8 -> x69, local copies, waits for them, and re-layouts: 0.14 us -> 39 us
  transfers between devices with their start and end apart: 3 -> 3, of which waited for: 2 -> 2; matrix products, arithmetic and copies ran while one was open for 11% -> 10% of each run, Pallas kernels for 0% -> 0%
where the time goes in v1:
time: 231 us
  waiting for transfers between devices  79.5 us (34%)
  local copies, waits for them, and re-layouts  62.2 us (27%)
  matrix products  31.3 us (14%)
  starting transfers between devices  17.4 us (8%)
  blocking collectives  14.1 us (6%)
  between operations  14.1 us (6%)
  other arithmetic  12.2 us (5%)
    all_to_all x1, waiting for transfers between devices, exchange_blocks(): blocks = lax.all_to_all(blocks, axis, split_axis=0, concat_axis=0)  51.1 us
    unnamed x69, local copies, waits for them, and re-layouts  39 us
    all_to_all x1, waiting for transfers between devices, turned_blocks(): lax.all_to_all(parts, axes[k], split_axis=k, concat_axis=k, tiled=True)  28.4 us
    scatter x1, local copies, waits for them, and re-layouts, body(): new_momentum = jnp.zeros_like(momentum).at[assignment].set(returned)  17.6 us
    dot_general x2, matrix products, newton_turn(): jnp.einsum('jfg,jgd->jfd', polynomial, iterate, preferred_element_type=jn...  15.7 us
    all_to_all x1, starting transfers between devices, exchange_blocks(): blocks = lax.all_to_all(blocks, axis, split_axis=0, concat_axis=0)  12.3 us
    dot_general x2, matrix products, body(): jnp.einsum('jfd,jgd->jfg', complete, complete, preferred_element_type=jnp...  11.6 us
    all_to_all x1, blocking collectives, from_everyone(): return lax.all_to_all(copies, axis, split_axis=0, concat_axis=0, tiled=True)  9.54 us
  transfers between devices with their start and end apart: 3, of which 2 were waited for; matrix products, arithmetic and copies ran while one was open for 10% of the time, Pallas kernels for 0%

profile of v1, /device:TPU:2, one launch (start us, length us, event | category | flops | bytes accessed | tf_op | source)
XLA Modules:
  0.0 230.8 jit_solution(6788831557335494142)
XLA Ops:
  7.2 0.8 compare_select_fusion
  8.0 0.7 compare_and_fusion
  8.8 2.1 gather_fusion
  10.9 1.8 broadcast_select_fusion
  12.7 0.6 constant_dynamic-update-slice_fusion.63
  13.9 0.6 constant_dynamic-update-slice_fusion.61
  21.3 0.6 constant_dynamic-update-slice_fusion.49
  52.2 12.3 %all-to-all-start = ((f32[64,2,8,512]{3,2,1,0:T(8,128)}), f32[64,2,8,512]{3,2,1,0:T(8,128)}, u32[]{:S(2)}, u32[]{:S(2)}) async-start(f32[64,2,8,512]{3,2,1,0:T(8,128)} %constant_dynamic-update-slice_fusion), calls=%async_computation | async-start | bytes 4194304 | tf_op jit(solution)/shard_map/all_to_all | solution.py:22
  64.6 51.1 %all-to-all-done = f32[64,2,8,512]{3,2,1,0:T(8,128)} async-done(((f32[64,2,8,512]{3,2,1,0:T(8,128)}), f32[64,2,8,512]{3,2,1,0:T(8,128)}, u32[]{:S(2)}, u32[]{:S(2)}) %all-to-all-start) | async-done | bytes 2097184 | tf_op jit(solution)/shard_map/all_to_all | solution.py:22
  115.7 3.9 %multiply_reduce_fusion = (f32[2]{0:T(128)S(1)}, f32[2,512,512]{2,1,0:T(8,128)}) fusion(bf16[512,512]{1,0:T(8,128)(2,1)S(1)} %copy-done.2, pred[512,2]{0,1:T(4,128)(4,1)S(1)} %iota_compare_fusion, bf16[512,512]{1,0:T(8,128)(2,1)} %param.7, f32[64,2,8,512]{3,2,1,0:T(8,128)} %all-to-all-done), kind=kOutput, calls=%fused_computation.10 | convolution fusion | flops 539492352 | bytes 5243912 | tf_op jit(solution)/shard_map/rf,rjd->jfd/dot_general | solution.py:80
  119.7 9.5 %all_to_all.21 = f32[4,1,2]{2,1,0:T(1,128)S(1)} all-to-all(f32[4,1,2]{2,1,0:T(1,128)S(1)} %broadcast_in_dim.50), channel_id=1, replica_groups=mesh['owner_0'=8,'owner_1'=4,'owner_2'=2,'col'=4] {'col'}, dimensions={0} | all-to-all | bytes 64 | tf_op jit(solution)/shard_map/all_to_all | solution.py:28
  129.2 3.6 %divide_convert_fusion = (bf16[2,512,512]{2,1,0:T(8,128)(2,1)}, bf16[2,512,512]{2,1,0:T(8,128)(2,1)S(1)}) fusion(f32[2,512,512]{2,1,0:T(8,128)} %get-tuple-element.5, f32[2]{0:T(128)S(1)} %sqrt_add_fusion), kind=kLoop, calls=%fused_computation.9 | loop fusion | flops 1572864 | bytes 4194312 | tf_op jit(solution)/shard_map/convert_element_type | solution.py:83
  133.1 4.6 %all_to_all.22 = bf16[32,2,2,8,512]{4,3,2,0,1:T(8,128)(2,1)S(1)} all-to-all(bf16[32,2,2,8,512]{4,3,2,0,1:T(8,128)(2,1)S(1)} %copy.28), channel_id=1, replica_groups=mesh['owner_0'=8,'owner_1'=4,'owner_2'=2,'col'=4] {'owner_2'}, dimensions={1} | all-to-all | bytes 2097152 | tf_op jit(solution)/shard_map/all_to_all | solution.py:51
  137.6 1.1 copy.29
  138.7 5.0 %all-to-all-start.2 = ((bf16[32,2,2,8,512]{4,3,2,1,0:T(8,128)(2,1)}), bf16[32,2,2,8,512]{4,3,2,1,0:T(8,128)(2,1)S(1)}, u32[]{:S(2)}, u32[]{:S(2)}) async-start(bf16[32,2,2,8,512]{4,3,2,1,0:T(8,128)(2,1)} %copy.29), calls=%async_computation.2 | async-start | bytes 2097152 | tf_op jit(solution)/shard_map/all_to_all | solution.py:51
  143.7 28.4 %all-to-all-done.2 = bf16[32,2,2,8,512]{4,3,2,1,0:T(8,128)(2,1)S(1)} async-done(((bf16[32,2,2,8,512]{4,3,2,1,0:T(8,128)(2,1)}), bf16[32,2,2,8,512]{4,3,2,1,0:T(8,128)(2,1)S(1)}, u32[]{:S(2)}, u32[]{:S(2)}) %all-to-all-start.2) | async-done | bytes 1048608 | tf_op jit(solution)/shard_map/all_to_all | solution.py:51
  172.1 1.7 bitcast_convert_fusion
  173.8 1.6 broadcast_in_dim.43
  175.4 17.6 %scatter_fusion = f32[128,8,512]{2,1,0:T(8,128)} fusion(f32[128,8,512]{2,1,0:T(8,128)} %broadcast_in_dim.43, s32[128]{0:T(128)S(1)} %compare_select_fusion, f32[128,8,512]{2,1,0:T(8,128)} %bitcast_convert_fusion), kind=kCustom, calls=%fused_computation.1 | custom fusion | bytes 6291968 | tf_op jit(solution)/shard_map/scatter | solution.py:95
  193.0 5.8 %convolution_convert_fusion.1 = bf16[2,512,512]{2,1,0:T(8,128)(2,1)S(1)} fusion(bf16[2,512,2048]{2,1,0:T(8,128)(2,1)} %all-gather.2.cloned.1.call-done), kind=kOutput, calls=%fused_computation.13 | convolution fusion | flops 2148007936 | bytes 5242880 | tf_op jit(solution)/shard_map/jfd,jgd->jfg/dot_general | solution.py:86
  198.8 7.3 %add_convert_fusion = bf16[2,512,2048]{2,1,0:T(8,128)(2,1)} fusion(bf16[2,512,2048]{2,1,0:T(8,128)(2,1)} %all-gather.2.cloned.1.call-done, bf16[2,512,512]{2,1,0:T(8,128)(2,1)S(1)} %convolution_convert_fusion.1), kind=kOutput, calls=%fused_computation.2 | convolution fusion | flops 2695364608 | bytes 9437184 | tf_op jit(solution)/shard_map/jfg,jgd->jfd/dot_general | solution.py:68
  206.2 5.8 %convolution_convert_fusion = bf16[2,512,512]{2,1,0:T(8,128)(2,1)S(1)} fusion(bf16[2,512,2048]{2,1,0:T(8,128)(2,1)} %add_convert_fusion), kind=kOutput, calls=%fused_computation.12 | convolution fusion | flops 2148007936 | bytes 5242880 | tf_op jit(solution)/shard_map/jfd,jgd->jfg/dot_general | solution.py:86
  212.0 8.3 %fusion.3 = f32[2,512,2048]{2,1,0:T(8,128)} fusion(bf16[2,512,2048]{2,1,0:T(8,128)(2,1)} %add_convert_fusion, bf16[2,512,512]{2,1,0:T(8,128)(2,1)S(1)} %convolution_convert_fusion), kind=kOutput, calls=%fused_computation.18 | convolution fusion | flops 2686976000 | bytes 13631488 | tf_op jit(solution)/shard_map/jfg,jgd->jfd/dot_general | solution.py:68
  220.3 3.6 %convert_multiply_fusion = f32[2,512,512]{2,1,0:T(8,128)} fusion(f32[2,512,2048]{2,1,0:T(8,128)} %fusion.3, s32[]{:T(128)S(6)} %select_n.20, bf16[2,512,2048]{2,1,0:T(8,128)(2,1)} %add_convert_fusion), kind=kLoop, calls=%fused_computation.6 | loop fusion | flops 3145728 | bytes 5242884 | tf_op jit(solution)/shard_map/mul | solution.py:91
  (76 shorter events, 38.0 us)
Async XLA Ops:
  7.2 1.6 copy-start
  52.2 12.4 %copy-start.1 = (s32[512]{0:T(512)S(1)}, s32[512]{0:T(512)}, u32[]{:S(2)}) copy-start(s32[512]{0:T(512)} %param.8) | copy-start | bytes 6148
  52.2 63.5 %copy-start.2 = (bf16[512,512]{1,0:T(8,128)(2,1)S(1)}, bf16[512,512]{1,0:T(8,128)(2,1)}, u32[]{:S(2)}) copy-start(bf16[512,512]{1,0:T(8,128)(2,1)} %param.6) | copy-start | bytes 1572868
  52.2 63.5 %all-to-all-start = ((f32[64,2,8,512]{3,2,1,0:T(8,128)}), f32[64,2,8,512]{3,2,1,0:T(8,128)}, u32[]{:S(2)}, u32[]{:S(2)}) async-start(f32[64,2,8,512]{3,2,1,0:T(8,128)} %constant_dynamic-update-slice_fusion), calls=%async_computation | async-start | bytes 4194304 | tf_op jit(solution)/shard_map/all_to_all | solution.py:22
  64.6 128.5 %all-gather.2.cloned.1.call-start = ((), (), s32[]{:S(2)}) async-start(), calls=%async_computation.4 | async-start | bytes 5242880 | tf_op jit(solution)/shard_map/all_gather | solution.py:84
  138.7 33.4 %all-to-all-start.2 = ((bf16[32,2,2,8,512]{4,3,2,1,0:T(8,128)(2,1)}), bf16[32,2,2,8,512]{4,3,2,1,0:T(8,128)(2,1)S(1)}, u32[]{:S(2)}, u32[]{:S(2)}) async-start(bf16[32,2,2,8,512]{4,3,2,1,0:T(8,128)(2,1)} %copy.29), calls=%async_computation.2 | async-start | bytes 2097152 | tf_op jit(solution)/shard_map/all_to_all | solution.py:51
Sparse Core Ops, SparseCore 0:
  133.0 45.1 all-gather.1
